TPU v7x, 32 devices: a whole 2x2x4 slice. The times are simulated.
32 devices in a mesh: grp: 1, date: 4 (over y, x), shard: 8 (over z, core).
Axes of the slice: x: 2, y: 2, z: 4, core: 2. Of those that a mesh axis runs over, the one named last changes fastest.
Arguments:
- echo_spectra: bfloat16 [4, 2, 128, 8192], P(('grp', 'date'), None, 'shard'), may hold values from -6 to 6
- range_reference: float32 [2, 8192], replicated, may hold values from -5 to 5
- azimuth_reference: bfloat16 [2, 128, 8192], P(None, None, 'shard'), may hold values from -5 to 5
- block_owner: int32 [4, 64], P(('grp', 'date')), may hold values from 0 to 7, as said below
- block_slot: int32 [4, 64], P(('grp', 'date')), may hold values from 0 to 15, as said below
- kernel_index: int32 [4, 64], P(('grp', 'date')), may hold values from 0 to 7
Outputs:
- filtered: bfloat16 [4, 128, 2, 2, 128, 128], P(('grp', 'date'), 'shard')
Inputs may be any that keep to these rules, and one draw needn't show every extreme that they name: `block_owner`: every date carries the same owners (the stack is coregistered onto one map grid). Within a date, the 8 blocks of one range-column group name any one owner at most 2 times, and some group names some owner exactly 2 times; every owner is named by at most 16 blocks, and some owner by exactly 16. `block_slot`: every date carries the same slots. Within a date, blocks that name the same owner have distinct slots.
All inputs are finite; a program needn't handle non-finite values.
Results may differ from a plain program's by a relative error of at most 0.017.
Values may be sent and summed in bfloat16 or wider, within the bound.
A program may use at most 128 MiB of HBM per device.

v0:
```python
import math
import jax
import jax.numpy as jnp
from jax import lax
from jax.sharding import PartitionSpec as P

RNG = 8192
RSPLIT = 64
BLK = 128
NSUB = 8
BLK_DEV = 8


def passed_along(value, axis, steps):
    count = lax.axis_size(axis)
    pairs = [(source, (source + steps) % count) for source in range(count)]
    return lax.ppermute(value, axis, pairs)


def dft_block(size, sign):
    index = jnp.arange(size, dtype=jnp.int32)
    phase = index[:, None] * index[None, :] % size
    angle = 2.0 * math.pi / size * phase.astype(jnp.float32)
    scale = 1.0 / math.sqrt(size)
    cosine = jnp.cos(angle) * scale
    sine = sign * jnp.sin(angle) * scale
    table = jnp.stack([jnp.stack([cosine, -sine]), jnp.stack([sine, cosine])])
    return jnp.transpose(table, (0, 2, 1, 3)).astype(jnp.bfloat16)


def twiddle(first_len, second_len, total):
    left = jnp.arange(first_len, dtype=jnp.int32)
    right = jnp.arange(second_len, dtype=jnp.int32)
    phase = left[:, None] * right[None, :] % total
    angle = 2.0 * math.pi / total * phase.astype(jnp.float32)
    return (jnp.cos(angle), jnp.sin(angle))


def kernel_table():
    offset = (jnp.arange(NSUB, dtype=jnp.float32) + 0.5) / NSUB
    cells = jnp.arange(BLK, dtype=jnp.float32)
    dist = cells[None, None, :] - cells[None, :, None] - offset[:, None, None]
    window = jnp.where(jnp.abs(dist) < 4.0, 0.5 + 0.5 * jnp.cos(math.pi * dist / 4.0), 0.0)
    return (jnp.sinc(dist) * window).astype(jnp.bfloat16)


def bdot(form, left, right):
    return jnp.einsum(form, left, right, preferred_element_type=jnp.float32)


def range_compress(spectra, reference):
    real_in = spectra[0].astype(jnp.float32)
    imag_in = spectra[1].astype(jnp.float32)
    matched = jnp.stack(
        [
            real_in * reference[0] + imag_in * reference[1],
            imag_in * reference[0] - real_in * reference[1],
        ]
    ).astype(jnp.bfloat16)
    count = spectra.shape[1]
    outer_len = RSPLIT
    inner_len = RNG // RSPLIT
    shaped = matched.reshape(2, count, outer_len, inner_len)
    section = bdot("cnek,epkb->cpnb", dft_block(outer_len, 1), shaped)
    twc, tws = twiddle(outer_len, inner_len, RNG)
    first = jnp.stack(
        [section[0] * twc - section[1] * tws, section[0] * tws + section[1] * twc]
    ).astype(jnp.bfloat16)
    second = bdot("cmek,epnk->cpmn", dft_block(inner_len, 1), first)
    return second.reshape(2, count, RNG).astype(jnp.bfloat16)


def azimuth_focus(columns, reference):
    count = columns.shape[1]
    doppler = bdot("cuep,epk->cuk", dft_block(count, -1), columns)
    ref_re = reference[0].astype(jnp.float32)
    ref_im = reference[1].astype(jnp.float32)
    shaped = jnp.stack(
        [doppler[0] * ref_re - doppler[1] * ref_im, doppler[0] * ref_im + doppler[1] * ref_re]
    ).astype(jnp.bfloat16)
    return bdot("cuep,epk->cuk", dft_block(count, 1), shaped).astype(jnp.bfloat16)


def resample(blocks, kinds):
    count = blocks.shape[0]
    picker = (kinds[:, None] == jnp.arange(NSUB, dtype=jnp.int32)[None, :]).astype(jnp.bfloat16)
    table = kernel_table().reshape(NSUB, BLK * BLK)
    kernels = (
        jnp.dot(picker, table, preferred_element_type=jnp.float32)
        .astype(jnp.bfloat16)
        .reshape(count, BLK, BLK)
    )
    return bdot("nij,ncjk->ncik", kernels, blocks).astype(jnp.bfloat16)


def cross(first, second):
    fre = first[:, 0].astype(jnp.float32)
    fim = first[:, 1].astype(jnp.float32)
    sre = second[:, 0].astype(jnp.float32)
    sim = second[:, 1].astype(jnp.float32)
    return jnp.stack([fre * sre + fim * sim, fim * sre - fre * sim], axis=1)


def goldstein(patches):
    forward = dft_block(BLK, -1)
    backward = dft_block(BLK, 1)
    rows = bdot("cuei,npeij->npcuj", forward, patches).astype(jnp.bfloat16)
    spectrum = bdot("npeuj,cvej->npcuv", rows, forward)
    power = spectrum[:, :, 0] ** 2 + spectrum[:, :, 1] ** 2
    smooth = jnp.zeros_like(power)
    for down in (-1, 0, 1):
        for across in (-1, 0, 1):
            smooth = smooth + jnp.roll(power, (down, across), axis=(-2, -1))
    smooth = smooth / 9.0
    level = jnp.mean(smooth, axis=(-2, -1), keepdims=True)
    weight = jnp.sqrt(jnp.sqrt(smooth / (level + 1e-06)))
    weighted = (spectrum * weight[:, :, None]).astype(jnp.bfloat16)
    back = bdot("cuei,npeij->npcuj", backward, weighted).astype(jnp.bfloat16)
    return bdot("npeuj,cvej->npcuv", back, backward).astype(jnp.bfloat16)


def body(echo_spectra, range_reference, azimuth_reference, block_owner, block_slot, kernel_index):
    shards = lax.axis_size("shard")
    most = max(2, 2 * BLK_DEV // shards)
    capacity = min(2 * BLK_DEV, shards * most)
    outgoing = shards * most
    compressed = range_compress(echo_spectra[0], range_reference)
    columns = lax.all_to_all(compressed, "shard", split_axis=2, concat_axis=1, tiled=True)
    image = azimuth_focus(columns, azimuth_reference)
    row_blocks = image.shape[1] // BLK
    col_blocks = image.shape[2] // BLK
    blocks = image.reshape(2, row_blocks, BLK, col_blocks, BLK)
    blocks = jnp.transpose(blocks, (1, 3, 0, 2, 4)).reshape(BLK_DEV, 2, BLK, BLK)
    owners = block_owner[0]
    slots = block_slot[0]
    kinds = kernel_index[0]
    total = owners.shape[0]
    me_index = lax.axis_index("shard")
    numbers = jnp.arange(total, dtype=jnp.int32)
    sender = numbers // BLK_DEV
    earlier = (
        (sender[:, None] == sender[None, :])
        & (owners[:, None] == owners[None, :])
        & (numbers[None, :] < numbers[:, None])
    )
    rank = jnp.sum(earlier.astype(jnp.int32), axis=1)
    target = owners * most + rank
    my_target = lax.dynamic_slice_in_dim(target, me_index * BLK_DEV, BLK_DEV)
    chooser = (my_target[None, :] == jnp.arange(outgoing, dtype=jnp.int32)[:, None]).astype(
        jnp.bfloat16
    )
    outbox = bdot("en,nxyz->exyz", chooser, blocks).astype(jnp.bfloat16)
    outbox = outbox.reshape(shards, most, 2, BLK, BLK)
    inbox = lax.all_to_all(outbox, "shard", split_axis=0, concat_axis=0, tiled=True).reshape(
        outgoing, 2, BLK, BLK
    )
    entry = sender * most + rank
    hits = owners == me_index
    slot_hit = (slots[None, :] == jnp.arange(capacity, dtype=jnp.int32)[:, None]) & hits[None, :]
    entry_hit = entry[:, None] == jnp.arange(outgoing, dtype=jnp.int32)[None, :]
    placing = jnp.dot(slot_hit.astype(jnp.float32), entry_hit.astype(jnp.float32)).astype(
        jnp.bfloat16
    )
    tile = bdot("qe,exyz->qxyz", placing, inbox).astype(jnp.bfloat16)
    slot_kinds = jnp.sum(slot_hit.astype(jnp.int32) * kinds[None, :], axis=1)
    tile = resample(tile, slot_kinds)
    following = passed_along(tile, "date", -1)
    second = passed_along(tile, "date", -2)
    pairs = jnp.stack([cross(tile, following), cross(tile, second)], axis=1).astype(jnp.bfloat16)
    return goldstein(pairs)[None]


def solution(mesh):
    in_specs = (
        P(("grp", "date"), None, "shard", None),
        P(),
        P(None, None, "shard"),
        P(("grp", "date"), None),
        P(("grp", "date"), None),
        P(("grp", "date"), None),
    )
    out_specs = P(("grp", "date"), "shard", None, None, None, None)
    return jax.shard_map(body, mesh=mesh, in_specs=in_specs, out_specs=out_specs, check_vma=False)
```

profile of v0, /device:TPU:2, one launch (start us, length us, event | category | flops | bytes accessed | tf_op | source)
XLA Modules:
  0.0 187.8 jit_solution(73576553824263236)
XLA Ops:
  0.0 0.2 negate_convert_fusion.2
  0.2 0.1 fusion.148
  0.3 0.1 fusion.153
  0.5 0.3 negate_convert_fusion
  0.7 0.3 multiply_convert_fusion.1
  1.0 0.3 multiply_convert_fusion.3
  1.3 1.1 convert_bitcast_fusion.1
  2.4 0.1 copy.148
  2.5 0.1 copy.149
  2.6 0.0 copy-done.5
  2.6 0.1 fusion.192
  2.7 0.2 fusion.84
  2.9 0.3 convolution_bitcast_fusion.1
  3.2 0.2 subtract_convert_fusion
  3.4 0.3 fusion.38
  3.8 5.6 %copy.128 = bf16[2,16,128,64]{1,0,3,2:T(2,128)(2,1)} copy(bf16[2,16,128,64]{2,3,0,1:T(8,128)(2,1)S(1)} %fusion.38) | data formatting | bytes 1048576 | tf_op jit(solution)/shard_map/convert_element_type | solution.py:70
  9.3 6.5 %reshape.594 = bf16[8,2,16384]{2,1,0:T(2,128)(2,1)} reshape(bf16[8192,2,16]{2,1,0:T(2,128)(2,1)} %bitcast.278) | data formatting | bytes 1048576
  15.8 4.9 %all-to-all-start = ((bf16[8,2,16384]{2,1,0:T(2,128)(2,1)}), bf16[8,2,16384]{2,1,0:T(2,128)(2,1)S(1)}, u32[]{:S(2)}, u32[]{:S(2)}) async-start(bf16[8,2,16384]{2,1,0:T(2,128)(2,1)} %reshape.594), calls=%async_computation | async-start | bytes 1048576 | tf_op jit(solution)/shard_map/all_to_all | solution.py:128
  20.7 0.2 convert_reduce_fusion
  20.9 0.1 dynamic_slice.3
  21.0 15.0 %all-to-all-done = bf16[8,2,16384]{2,1,0:T(2,128)(2,1)S(1)} async-done(((bf16[8,2,16384]{2,1,0:T(2,128)(2,1)}), bf16[8,2,16384]{2,1,0:T(2,128)(2,1)S(1)}, u32[]{:S(2)}, u32[]{:S(2)}) %all-to-all-start) | async-done | bytes 524320 | tf_op jit(solution)/shard_map/all_to_all | solution.py:128
  36.0 4.1 %reshape.595 = bf16[8192,2,16]{2,1,0:T(2,128)(2,1)} reshape(bf16[8,2,16384]{2,1,0:T(2,128)(2,1)S(1)} %all-to-all-done) | data formatting | bytes 1048576
  40.1 9.0 %copy.130 = bf16[2,16,8,1024]{3,1,2,0:T(8,128)(2,1)S(1)} copy(bf16[2,16,8,1024]{1,0,3,2:T(2,128)(2,1)} %bitcast.279) | data formatting | bytes 1048576 | tf_op jit(solution)/shard_map/all_to_all | solution.py:128
  49.0 0.3 convolution_bitcast_fusion.3
  49.4 0.2 fusion.56
  49.6 0.3 fusion.37
  49.9 0.1 copy.150
  50.0 0.5 convolution_convert_fusion.2
  50.5 0.0 copy-start.7
  50.5 0.0 copy-start.8
  50.5 2.0 %copy.79 = bf16[8,2,2,128,128]{4,1,3,2,0:T(2,128)(2,1)} copy(bf16[8,2,2,128,128]{4,1,0,3,2:T(2,128)(2,1)S(1)} %bitcast.281) | data formatting | bytes 2097152 | tf_op jit(solution)/shard_map/reshape | solution.py:153
  52.5 3.6 %all-to-all-start.1 = ((bf16[8,2,2,128,128]{4,1,3,2,0:T(2,128)(2,1)}), bf16[8,2,2,128,128]{4,1,3,2,0:T(2,128)(2,1)S(1)}, u32[]{:S(2)}, u32[]{:S(2)}) async-start(bf16[8,2,2,128,128]{4,1,3,2,0:T(2,128)(2,1)} %copy.79), calls=%async_computation.1 | async-start | bytes 2097152 | tf_op jit(solution)/shard_map/all_to_all | solution.py:154
  56.1 0.1 select_reduce_fusion
  56.3 2.8 %fusion.39 = bf16[2,8,128,128]{3,1,2,0:T(8,128)(2,1)S(1)} fusion(f32[8]{0:T(128)S(1)} %add_multiply_fusion, f32[16384]{0:T(1024)S(1)} %subtract_bitcast_fusion, s32[16]{0:T(128)S(1)} %select_reduce_fusion), kind=kOutput, calls=%fused_computation.74 | convolution fusion | flops 9830528 | bytes 589920 | tf_op jit(solution)/shard_map/dot_general | solution.py:89
  59.1 0.1 copy.151
  59.2 23.4 %all-to-all-done.1 = bf16[8,2,2,128,128]{4,1,3,2,0:T(2,128)(2,1)S(1)} async-done(((bf16[8,2,2,128,128]{4,1,3,2,0:T(2,128)(2,1)}), bf16[8,2,2,128,128]{4,1,3,2,0:T(2,128)(2,1)S(1)}, u32[]{:S(2)}, u32[]{:S(2)}) %all-to-all-start.1) | async-done | bytes 1048608 | tf_op jit(solution)/shard_map/all_to_all | solution.py:154
  82.6 0.7 copy.80
  83.3 0.6 convolution_convert_fusion.1
  83.9 0.5 fusion.35
  84.4 0.8 collective-permute-start
  85.2 1.5 collective-permute-start.1
  86.7 23.6 %collective-permute-done = bf16[16,2,128,128]{2,3,1,0:T(8,128)(2,1)S(1)} collective-permute-done((bf16[16,2,128,128]{2,3,1,0:T(8,128)(2,1)S(1)}, bf16[16,2,128,128]{2,3,1,0:T(8,128)(2,1)S(1)}, u32[]{:S(2)}, u32[]{:S(2)}) %collective-permute-start) | collective-permute-done | bytes 1048608 | tf_op jit(solution)/shard_map/ppermute | solution.py:17
  110.3 21.7 %collective-permute-done.1 = bf16[16,2,128,128]{2,3,1,0:T(8,128)(2,1)S(1)} collective-permute-done((bf16[16,2,128,128]{2,3,1,0:T(8,128)(2,1)S(1)}, bf16[16,2,128,128]{2,3,1,0:T(8,128)(2,1)S(1)}, u32[]{:S(2)}, u32[]{:S(2)}) %collective-permute-start.1) | collective-permute-done | bytes 1048608 | tf_op jit(solution)/shard_map/ppermute | solution.py:17
  132.0 1.0 fusion.45
  133.0 0.1 maximum_bitcast_fusion.1
  133.1 0.1 maximum_bitcast_fusion.2
  133.2 3.4 %convolution_bitcast_fusion = f32[16,2,2,128,128]{3,4,1,0,2:T(8,128)} fusion(bf16[1,2,128,128]{3,2,1,0:T(8,128)(2,1)S(1)} %get-tuple-element.44, bf16[1,2,128,128]{3,2,1,0:T(8,128)(2,1)S(1)} %get-tuple-element.43, bf16[16,1,2,128,128]{3,4,2,0,1:T(8,128)(2,1)S(1)} %maximum_bitcast_fusion.2, bf16[16,1,2,128,128]{3,4,2,0,1:T(8,128)(2,1)S(1)} %maximum_bitcast_fusion.1), kind=kOutput, calls=%fused_computation.5 | convolution fusion | flops 1076363264 | bytes 6422528 | tf_op jit(solution)/shard_map/npeuj,cvej->npcuv/dot_general | solution.py:48
  136.7 2.5 %fusion.96 = f32[16,2,128,128]{2,3,1,0:T(8,128)S(1)} fusion(f32[16,2,2,128,128]{3,4,1,0,2:T(8,128)} %convolution_bitcast_fusion), kind=kLoop, calls=%fused_computation.151 | loop fusion | flops 1572864 | bytes 6291456 | tf_op jit(solution)/shard_map/add | solution.py:109
  139.2 3.0 %slice_bitcast_fusion.5 = (f32[16,2,1,127,128]{3,4,1,0,2:T(8,128)}, f32[16,2,1,127,128]{3,4,1,0,2:T(8,128)}, f32[16,2,127,128]{2,3,1,0:T(8,128)S(1)}, f32[16,2,127,128]{2,3,1,0:T(8,128)S(1)}) fusion(f32[16,2,128,128]{2,3,1,0:T(8,128)S(1)} %fusion.96), kind=kLoop, calls=%fused_computation.281 | loop fusion | bytes 12484608 | tf_op jit(solution)/shard_map/jit(_roll_static)/concatenate | solution.py:113
  142.2 0.7 fusion.191
  143.0 0.1 fusion.151
  143.1 0.5 copy-done.2
  143.6 3.2 %slice_maximum_fusion.3 = (f32[16,2,128,127]{2,3,1,0:T(8,128)}, f32[16,2,128,127]{2,3,1,0:T(8,128)}) fusion(f32[16,2,1,128]{2,3,1,0:T(8,128)S(1)} %get-tuple-element.25, f32[16,2,127,128]{2,3,1,0:T(8,128)S(1)} %get-tuple-element.24), kind=kLoop, calls=%fused_computation.10 | loop fusion | flops 1040384 | bytes 6258688 | tf_op jit(solution)/shard_map/jit(_roll_static)/concatenate | solution.py:113
  146.8 0.1 fusion.149
  146.9 3.3 %slice_maximum_fusion.1 = (f32[16,2,128,127]{2,3,1,0:T(8,128)}, f32[16,2,128,127]{2,3,1,0:T(8,128)}) fusion(f32[16,2,127,128]{2,3,1,0:T(8,128)S(1)} %get-tuple-element.23, f32[16,2,1,128]{2,3,1,0:T(8,128)S(1)} %get-tuple-element.26), kind=kLoop, calls=%fused_computation.8 | loop fusion | flops 1040384 | bytes 6258688 | tf_op jit(solution)/shard_map/jit(_roll_static)/concatenate | solution.py:113
  150.2 4.0 %fusion.189 = (f32[16,2,128,127]{2,3,1,0:T(8,128)}, f32[16,2,1,128,127]{3,4,1,0,2:T(8,128)}, f32[16,2,1,128,127]{3,4,1,0,2:T(8,128)}, f32[16,2,128,127]{2,3,1,0:T(8,128)}) fusion(f32[16,2,128,128]{2,3,1,0:T(8,128)S(1)} %fusion.96), kind=kLoop, calls=%fused_computation.282 | loop fusion | bytes 12484608 | tf_op jit(solution)/shard_map/jit(_roll_static)/slice | solution.py:113
  154.3 2.2 %copy.99 = f32[16,2,1,128]{3,0,2,1:T(8,128)S(1)} copy(f32[16,2,1,128]{2,3,1,0:T(8,128)} %copy-done) | data formatting | bytes 32768 | tf_op jit(solution)/shard_map/jit(_roll_static)/slice | solution.py:113
  156.5 0.6 copy.88
  157.1 9.2 %fusion.23 = f32[16,2]{1,0:T(8,128)S(1)} fusion(f32[16,2,128,127]{2,3,1,0:T(8,128)} %get-tuple-element.10, f32[16,2,128,1]{2,3,1,0:T(1,128)S(1)} %get-tuple-element.12, f32[16,2,128,1]{2,3,1,0:T(1,128)S(1)} %get-tuple-element.11, f32[16,2,128,127]{2,3,1,0:T(8,128)} %get-tuple-element.9, f32[16,2,128,127]{2,3,1,0:T(8,128)} %get-tuple-element.16, ...), kind=kLoop, calls=%fused_computation.39 | loop fusion | flops 11010016 | bytes 20971648 | tf_op jit(solution)/shard_map/reduce_sum | solution.py:115
  166.3 1.9 %copy.100 = f32[16,2,1,1,128]{3,4,1,0,2:T(8,128)} copy(f32[16,2,1,1,128]{4,0,3,2,1:T(8,128)S(1)} %bitcast.293) | data formatting | bytes 32768 | tf_op jit(solution)/shard_map/jit(_roll_static)/concatenate | solution.py:113
  168.2 2.0 %copy.89 = f32[16,2,1,1,128]{3,4,1,0,2:T(8,128)} copy(f32[16,2,1,1,128]{4,0,3,2,1:T(8,128)S(1)} %bitcast.292) | data formatting | bytes 32768 | tf_op jit(solution)/shard_map/jit(_roll_static)/concatenate | solution.py:113
  170.3 10.6 %sqrt_bitcast_fusion = f32[16,2,128,128]{2,3,1,0:T(8,128)} fusion(f32[16,2,1,128,127]{3,4,1,0,2:T(8,128)} %bitcast.277, f32[16,2,1,128,1]{3,4,1,0,2:T(1,128)S(1)} %bitcast.289, f32[16,2,1,127,128]{3,4,1,0,2:T(8,128)} %get-tuple-element.22, f32[16,2,1,1,128]{3,4,1,0,2:T(8,128)} %copy.100, f32[16,2,1,128,1]{3,4,1,0,2:T(1,128)S(1)} %bitcast.288, ...), kind=kLoop, calls=%fused_computation.38 | loop fusion | flops 11010048 | bytes 23068800 | tf_op jit(solution)/shard_map/mul | solution.py:117
  180.8 4.3 %fusion.24 = bf16[1,16,2,2,128,128]{4,5,2,1,3,0:T(8,128)(2,1)S(1)} fusion(bf16[1,2,128,128]{3,2,1,0:T(8,128)(2,1)S(1)} %get-tuple-element.45, bf16[1,2,128,128]{3,2,1,0:T(8,128)(2,1)S(1)} %get-tuple-element.46, f32[16,2,2,128,128]{3,4,1,0,2:T(8,128)} %convolution_bitcast_fusion, f32[16,2,128,128]{2,3,1,0:T(8,128)} %sqrt_bitcast_fusion), kind=kOutput, calls=%fused_computation.54 | convolution fusion | flops 1078460416 | bytes 8519680 | tf_op jit(solution)/shard_map/npeuj,cvej->npcuv/dot_general | solution.py:48
  185.2 2.6 %copy.106 = bf16[1,16,2,2,128,128]{5,4,3,2,1,0:T(8,128)(2,1)} copy(bf16[1,16,2,2,128,128]{4,5,2,1,3,0:T(8,128)(2,1)S(1)} %fusion.24) | data formatting | bytes 4194304 | tf_op jit(solution)/shard_map/broadcast_in_dim | solution.py:170
  (23 shorter events, 0.2 us)
Async XLA Ops:
  0.0 2.6 %copy-start.5 = (f32[2,8192]{1,0:T(2,128)S(1)}, f32[2,8192]{1,0:T(2,128)}, u32[]{:S(2)}) copy-start(f32[2,8192]{1,0:T(2,128)} %param.7) | copy-start | bytes 196612
  9.3 11.4 %copy-start.6 = (s32[1,64]{1,0:T(1,128)S(1)}, s32[1,64]{1,0:T(1,128)}, u32[]{:S(2)}) copy-start(s32[1,64]{1,0:T(1,128)} %param.9) | copy-start | bytes 772
  15.8 20.2 %all-to-all-start = ((bf16[8,2,16384]{2,1,0:T(2,128)(2,1)}), bf16[8,2,16384]{2,1,0:T(2,128)(2,1)S(1)}, u32[]{:S(2)}, u32[]{:S(2)}) async-start(bf16[8,2,16384]{2,1,0:T(2,128)(2,1)} %reshape.594), calls=%async_computation | async-start | bytes 1048576 | tf_op jit(solution)/shard_map/all_to_all | solution.py:128
  40.1 9.3 %copy-start.4 = (bf16[2,128,1024]{2,1,0:T(8,128)(2,1)S(1)}, bf16[2,128,1024]{2,1,0:T(8,128)(2,1)}, u32[]{:S(2)}) copy-start(bf16[2,128,1024]{2,1,0:T(8,128)(2,1)} %param.8) | copy-start | bytes 1572868
  50.5 5.6 %copy-start.7 = (s32[1,64]{1,0:T(1,128)S(1)}, s32[1,64]{1,0:T(1,128)}, u32[]{:S(2)}) copy-start(s32[1,64]{1,0:T(1,128)} %param.10) | copy-start | bytes 772
  50.5 5.6 %copy-start.8 = (s32[1,64]{1,0:T(1,128)S(1)}, s32[1,64]{1,0:T(1,128)}, u32[]{:S(2)}) copy-start(s32[1,64]{1,0:T(1,128)} %param.11) | copy-start | bytes 772
  52.5 30.1 %all-to-all-start.1 = ((bf16[8,2,2,128,128]{4,1,3,2,0:T(2,128)(2,1)}), bf16[8,2,2,128,128]{4,1,3,2,0:T(2,128)(2,1)S(1)}, u32[]{:S(2)}, u32[]{:S(2)}) async-start(bf16[8,2,2,128,128]{4,1,3,2,0:T(2,128)(2,1)} %copy.79), calls=%async_computation.1 | async-start | bytes 2097152 | tf_op jit(solution)/shard_map/all_to_all | solution.py:154
  84.4 25.8 %collective-permute-start = (bf16[16,2,128,128]{2,3,1,0:T(8,128)(2,1)S(1)}, bf16[16,2,128,128]{2,3,1,0:T(8,128)(2,1)S(1)}, u32[]{:S(2)}, u32[]{:S(2)}) collective-permute-start(bf16[16,2,128,128]{2,3,1,0:T(8,128)(2,1)S(1)} %fusion.35), channel_id=1, source_target_pairs={{0,24},{8,0},{16,8},{24,16},{1,25},{9,1},{17,9},{25,17},{2,26},{10... | collective-permute-start | bytes 3145736 | tf_op jit(solution)/shard_map/ppermute | solution.py:17
  85.2 46.8 %collective-permute-start.1 = (bf16[16,2,128,128]{2,3,1,0:T(8,128)(2,1)S(1)}, bf16[16,2,128,128]{2,3,1,0:T(8,128)(2,1)S(1)}, u32[]{:S(2)}, u32[]{:S(2)}) collective-permute-start(bf16[16,2,128,128]{2,3,1,0:T(8,128)(2,1)S(1)} %fusion.35), channel_id=1, source_target_pairs={{0,16},{8,24},{16,0},{24,8},{1,17},{9,25},{17,1},{25,9},{2,18},{10... | collective-permute-start | bytes 3145736 | tf_op jit(solution)/shard_map/ppermute | solution.py:17
  142.2 1.4 copy-start.2
  142.2 4.7 %copy-start.1 = (f32[16,2,127,128]{2,3,1,0:T(8,128)}, f32[16,2,127,128]{2,3,1,0:T(8,128)S(1)}, u32[]{:S(2)}) copy-start(f32[16,2,127,128]{2,3,1,0:T(8,128)S(1)} %get-tuple-element.23) | copy-start | bytes 6242308
  143.0 4.0 %copy-start = (f32[16,2,1,128]{2,3,1,0:T(8,128)}, f32[16,2,1,128]{2,3,1,0:T(8,128)S(1)}, u32[]{:S(2)}) copy-start(f32[16,2,1,128]{2,3,1,0:T(8,128)S(1)} %get-tuple-element.26) | copy-start | bytes 49156
  166.3 4.0 %copy-start.3 = (f32[16,2,128,127]{2,3,1,0:T(8,128)S(1)}, f32[16,2,128,127]{2,3,1,0:T(8,128)}, u32[]{:S(2)}) copy-start(f32[16,2,128,127]{2,3,1,0:T(8,128)} %get-tuple-element.5) | copy-start | bytes 6242308
where the time goes:
time: 188 us
  waiting for transfers between devices  83.7 us (45%)
  local copies, waits for them, and re-layouts  46 us (24%)
  other arithmetic  33.5 us (18%)
  matrix products  13.5 us (7%)
  starting transfers between devices  10.7 us (6%)
    ppermute x2, waiting for transfers between devices, passed_along(): return lax.ppermute(value, axis, pairs)  45.3 us
    all_to_all x1, waiting for transfers between devices, body(): lax.all_to_all(outbox, 'shard', split_axis=0, concat_axis=0, tiled=True)  23.4 us
    all_to_all x1, waiting for transfers between devices, body(): lax.all_to_all(compressed, 'shard', split_axis=2, concat_axis=1, tiled=True)  15 us
    unnamed x24, local copies, waits for them, and re-layouts  11.4 us
    dot_general x9, matrix products, bdot(): return jnp.einsum(form, left, right, preferred_element_type=jnp.float32)  10.7 us
    mul x1, other arithmetic, goldstein(): weighted = (spectrum * weight[:, :, None]).astype(jnp.bfloat16)  10.6 us
    reduce_sum x1, other arithmetic, goldstein(): level = jnp.mean(smooth, axis=(-2, -1), keepdims=True)  9.16 us
    all_to_all x1, local copies, waits for them, and re-layouts, body(): lax.all_to_all(compressed, 'shard', split_axis=2, concat_axis=1, tiled=True)  8.96 us
  transfers between devices with their start and end apart: 4, of which 4 were waited for; matrix products, arithmetic and copies ran while one was open for 2% of the time, Pallas kernels for 0%

commit v1 on v0

--- a/solution.py
+++ b/solution.py
@@ -125,7 +125,12 @@
     capacity = min(2 * BLK_DEV, shards * most)
     outgoing = shards * most
     compressed = range_compress(echo_spectra[0], range_reference)
-    columns = lax.all_to_all(compressed, "shard", split_axis=2, concat_axis=1, tiled=True)
+    columns = jnp.concatenate(
+        lax.all_to_all(
+            jnp.stack(jnp.split(compressed, lax.axis_size("shard"), axis=2)), "shard", 0, 0
+        ),
+        axis=1,
+    )
     image = azimuth_focus(columns, azimuth_reference)
     row_blocks = image.shape[1] // BLK
     col_blocks = image.shape[2] // BLK

time: 188 us -> 169 us (0.90)
  local copies, waits for them, and re-layouts: 46 us -> 27.3 us
    all_to_all x1 -> x0, local copies, waits for them, and re-layouts: 8.96 us -> none  [body(): lax.all_to_all(compressed, 'shard', split_axis=2, concat_axis=1, tiled=True)]
    unnamed x24 -> x29, local copies, waits for them, and re-layouts: 11.4 us -> 5.34 us
    convert_element_type x1 -> x2, local copies, waits for them, and re-layouts: 5.57 us -> 1.3 us  [range_compress(): return second.reshape(2, count, RNG).astype(jnp.bfloat16)]
where the time goes in v1:
time: 169 us
  waiting for transfers between devices  83.7 us (50%)
  other arithmetic  33.5 us (20%)
  local copies, waits for them, and re-layouts  27.3 us (16%)
  matrix products  13.5 us (8%)
  starting transfers between devices  10.7 us (6%)
    ppermute x2, waiting for transfers between devices, passed_along(): return lax.ppermute(value, axis, pairs)  45.3 us
    all_to_all x1, waiting for transfers between devices, body(): lax.all_to_all(outbox, 'shard', split_axis=0, concat_axis=0, tiled=True)  23.4 us
    all_to_all x1, waiting for transfers between devices, body(): lax.all_to_all(jnp.stack(jnp.split(compressed, lax.axis_size('shard'), ax...  15 us
    dot_general x9, matrix products, bdot(): return jnp.einsum(form, left, right, preferred_element_type=jnp.float32)  10.7 us
    mul x1, other arithmetic, goldstein(): weighted = (spectrum * weight[:, :, None]).astype(jnp.bfloat16)  10.6 us
    reduce_sum x1, other arithmetic, goldstein(): level = jnp.mean(smooth, axis=(-2, -1), keepdims=True)  9.16 us
    slice x5, local copies, waits for them, and re-layouts, goldstein(): smooth = smooth + jnp.roll(power, (down, across), axis=(-2, -1))  7.63 us
    concatenate x3, local copies, waits for them, and re-layouts, goldstein(): smooth = smooth + jnp.roll(power, (down, across), axis=(-2, -1))  6.95 us
  transfers between devices with their start and end apart: 4, of which 4 were waited for; matrix products, arithmetic and copies ran while one was open for 2% of the time, Pallas kernels for 0%

profile of v1, /device:TPU:2, one launch (start us, length us, event | category | flops | bytes accessed | tf_op | source)
XLA Modules:
  0.0 169.1 jit_solution(16456775039508118923)
XLA Ops:
  0.0 0.2 negate_convert_fusion.2
  0.2 0.1 fusion.156
  0.3 0.1 fusion.161
  0.5 0.3 negate_convert_fusion
  0.7 0.3 multiply_convert_fusion.1
  1.0 0.3 multiply_convert_fusion.3
  1.3 1.1 convert_bitcast_fusion.1
  2.4 0.1 copy.147
  2.5 0.1 copy.148
  2.7 0.2 fusion.84
  2.9 0.3 convolution_bitcast_fusion.1
  3.2 0.2 subtract_convert_fusion
  3.4 0.3 fusion.38
  3.8 0.5 copy.80
  4.3 0.8 convert_element_type.270
  5.1 0.6 fusion.136
  5.7 0.6 fusion.135
  6.3 0.6 fusion.134
  7.0 0.6 fusion.133
  7.6 0.6 fusion.132
  8.2 0.6 fusion.131
  8.9 0.6 fusion.130
  9.5 0.6 fusion.129
  10.2 4.9 %all-to-all-start = ((bf16[8,2,16,1024]{3,2,1,0:T(8,128)(2,1)}), bf16[8,2,16,1024]{3,2,1,0:T(8,128)(2,1)S(1)}, u32[]{:S(2)}, u32[]{:S(2)}) async-start(bf16[8,2,16,1024]{3,2,1,0:T(8,128)(2,1)} %fusion.129), calls=%async_computation | async-start | bytes 1048576 | tf_op jit(solution)/shard_map/all_to_all | solution.py:129
  15.0 0.2 convert_reduce_fusion
  15.3 15.0 %all-to-all-done = bf16[8,2,16,1024]{3,2,1,0:T(8,128)(2,1)S(1)} async-done(((bf16[8,2,16,1024]{3,2,1,0:T(8,128)(2,1)}), bf16[8,2,16,1024]{3,2,1,0:T(8,128)(2,1)S(1)}, u32[]{:S(2)}, u32[]{:S(2)}) %all-to-all-start) | async-done | bytes 524320 | tf_op jit(solution)/shard_map/all_to_all | solution.py:129
  30.4 0.3 convolution_bitcast_fusion.3
  30.7 0.2 fusion.56
  30.9 0.3 fusion.37
  31.3 0.5 convolution_convert_fusion.2
  31.9 2.0 %copy.82 = bf16[8,2,2,128,128]{4,1,3,2,0:T(2,128)(2,1)} copy(bf16[8,2,2,128,128]{4,1,0,3,2:T(2,128)(2,1)S(1)} %bitcast.307) | data formatting | bytes 2097152 | tf_op jit(solution)/shard_map/reshape | solution.py:158
  33.9 3.6 %all-to-all-start.1 = ((bf16[8,2,2,128,128]{4,1,3,2,0:T(2,128)(2,1)}), bf16[8,2,2,128,128]{4,1,3,2,0:T(2,128)(2,1)S(1)}, u32[]{:S(2)}, u32[]{:S(2)}) async-start(bf16[8,2,2,128,128]{4,1,3,2,0:T(2,128)(2,1)} %copy.82), calls=%async_computation.1 | async-start | bytes 2097152 | tf_op jit(solution)/shard_map/all_to_all | solution.py:159
  37.5 0.1 select_reduce_fusion
  37.6 2.8 %fusion.39 = bf16[2,8,128,128]{3,1,2,0:T(8,128)(2,1)S(1)} fusion(f32[8]{0:T(128)S(1)} %add_multiply_fusion, f32[16384]{0:T(1024)S(1)} %subtract_bitcast_fusion, s32[16]{0:T(128)S(1)} %select_reduce_fusion), kind=kOutput, calls=%fused_computation.74 | convolution fusion | flops 9830528 | bytes 589920 | tf_op jit(solution)/shard_map/dot_general | solution.py:89
  40.5 0.1 copy.150
  40.6 23.4 %all-to-all-done.1 = bf16[8,2,2,128,128]{4,1,3,2,0:T(2,128)(2,1)S(1)} async-done(((bf16[8,2,2,128,128]{4,1,3,2,0:T(2,128)(2,1)}), bf16[8,2,2,128,128]{4,1,3,2,0:T(2,128)(2,1)S(1)}, u32[]{:S(2)}, u32[]{:S(2)}) %all-to-all-start.1) | async-done | bytes 1048608 | tf_op jit(solution)/shard_map/all_to_all | solution.py:159
  63.9 0.7 copy.83
  64.7 0.6 convolution_convert_fusion.1
  65.3 0.5 fusion.35
  65.8 0.8 collective-permute-start
  66.5 1.5 collective-permute-start.1
  68.1 23.6 %collective-permute-done = bf16[16,2,128,128]{2,3,1,0:T(8,128)(2,1)S(1)} collective-permute-done((bf16[16,2,128,128]{2,3,1,0:T(8,128)(2,1)S(1)}, bf16[16,2,128,128]{2,3,1,0:T(8,128)(2,1)S(1)}, u32[]{:S(2)}, u32[]{:S(2)}) %collective-permute-start) | collective-permute-done | bytes 1048608 | tf_op jit(solution)/shard_map/ppermute | solution.py:17
  91.6 21.7 %collective-permute-done.1 = bf16[16,2,128,128]{2,3,1,0:T(8,128)(2,1)S(1)} collective-permute-done((bf16[16,2,128,128]{2,3,1,0:T(8,128)(2,1)S(1)}, bf16[16,2,128,128]{2,3,1,0:T(8,128)(2,1)S(1)}, u32[]{:S(2)}, u32[]{:S(2)}) %collective-permute-start.1) | collective-permute-done | bytes 1048608 | tf_op jit(solution)/shard_map/ppermute | solution.py:17
  113.3 1.0 fusion.45
  114.4 0.1 maximum_bitcast_fusion.1
  114.5 0.1 maximum_bitcast_fusion.2
  114.6 3.4 %convolution_bitcast_fusion = f32[16,2,2,128,128]{3,4,1,0,2:T(8,128)} fusion(bf16[1,2,128,128]{3,2,1,0:T(8,128)(2,1)S(1)} %get-tuple-element.44, bf16[1,2,128,128]{3,2,1,0:T(8,128)(2,1)S(1)} %get-tuple-element.43, bf16[16,1,2,128,128]{3,4,2,0,1:T(8,128)(2,1)S(1)} %maximum_bitcast_fusion.2, bf16[16,1,2,128,128]{3,4,2,0,1:T(8,128)(2,1)S(1)} %maximum_bitcast_fusion.1), kind=kOutput, calls=%fused_computation.5 | convolution fusion | flops 1076363264 | bytes 6422528 | tf_op jit(solution)/shard_map/npeuj,cvej->npcuv/dot_general | solution.py:48
  118.0 2.5 %fusion.96 = f32[16,2,128,128]{2,3,1,0:T(8,128)S(1)} fusion(f32[16,2,2,128,128]{3,4,1,0,2:T(8,128)} %convolution_bitcast_fusion), kind=kLoop, calls=%fused_computation.151 | loop fusion | flops 1572864 | bytes 6291456 | tf_op jit(solution)/shard_map/add | solution.py:109
  120.6 3.0 %slice_bitcast_fusion.13 = (f32[16,2,1,127,128]{3,4,1,0,2:T(8,128)}, f32[16,2,1,127,128]{3,4,1,0,2:T(8,128)}, f32[16,2,127,128]{2,3,1,0:T(8,128)S(1)}, f32[16,2,127,128]{2,3,1,0:T(8,128)S(1)}) fusion(f32[16,2,128,128]{2,3,1,0:T(8,128)S(1)} %fusion.96), kind=kLoop, calls=%fused_computation.297 | loop fusion | bytes 12484608 | tf_op jit(solution)/shard_map/jit(_roll_static)/concatenate | solution.py:113
  123.6 0.7 fusion.199
  124.3 0.1 fusion.159
  124.5 0.5 copy-done.2
  124.9 3.2 %slice_maximum_fusion.3 = (f32[16,2,128,127]{2,3,1,0:T(8,128)}, f32[16,2,128,127]{2,3,1,0:T(8,128)}) fusion(f32[16,2,1,128]{2,3,1,0:T(8,128)S(1)} %get-tuple-element.25, f32[16,2,127,128]{2,3,1,0:T(8,128)S(1)} %get-tuple-element.24), kind=kLoop, calls=%fused_computation.10 | loop fusion | flops 1040384 | bytes 6258688 | tf_op jit(solution)/shard_map/jit(_roll_static)/concatenate | solution.py:113
  128.1 0.1 fusion.157
  128.3 3.3 %slice_maximum_fusion.1 = (f32[16,2,128,127]{2,3,1,0:T(8,128)}, f32[16,2,128,127]{2,3,1,0:T(8,128)}) fusion(f32[16,2,127,128]{2,3,1,0:T(8,128)S(1)} %get-tuple-element.23, f32[16,2,1,128]{2,3,1,0:T(8,128)S(1)} %get-tuple-element.26), kind=kLoop, calls=%fused_computation.8 | loop fusion | flops 1040384 | bytes 6258688 | tf_op jit(solution)/shard_map/jit(_roll_static)/concatenate | solution.py:113
  131.6 4.0 %fusion.197 = (f32[16,2,128,127]{2,3,1,0:T(8,128)}, f32[16,2,1,128,127]{3,4,1,0,2:T(8,128)}, f32[16,2,1,128,127]{3,4,1,0,2:T(8,128)}, f32[16,2,128,127]{2,3,1,0:T(8,128)}) fusion(f32[16,2,128,128]{2,3,1,0:T(8,128)S(1)} %fusion.96), kind=kLoop, calls=%fused_computation.298 | loop fusion | bytes 12484608 | tf_op jit(solution)/shard_map/jit(_roll_static)/slice | solution.py:113
  135.6 2.2 %copy.102 = f32[16,2,1,128]{3,0,2,1:T(8,128)S(1)} copy(f32[16,2,1,128]{2,3,1,0:T(8,128)} %copy-done) | data formatting | bytes 32768 | tf_op jit(solution)/shard_map/jit(_roll_static)/slice | solution.py:113
  137.8 0.6 copy.91
  138.5 9.2 %fusion.23 = f32[16,2]{1,0:T(8,128)S(1)} fusion(f32[16,2,128,127]{2,3,1,0:T(8,128)} %get-tuple-element.10, f32[16,2,128,1]{2,3,1,0:T(1,128)S(1)} %get-tuple-element.12, f32[16,2,128,1]{2,3,1,0:T(1,128)S(1)} %get-tuple-element.11, f32[16,2,128,127]{2,3,1,0:T(8,128)} %get-tuple-element.9, f32[16,2,128,127]{2,3,1,0:T(8,128)} %get-tuple-element.16, ...), kind=kLoop, calls=%fused_computation.39 | loop fusion | flops 11010016 | bytes 20971648 | tf_op jit(solution)/shard_map/reduce_sum | solution.py:115
  147.7 1.9 %copy.103 = f32[16,2,1,1,128]{3,4,1,0,2:T(8,128)} copy(f32[16,2,1,1,128]{4,0,3,2,1:T(8,128)S(1)} %bitcast.320) | data formatting | bytes 32768 | tf_op jit(solution)/shard_map/jit(_roll_static)/concatenate | solution.py:113
  149.6 2.0 %copy.92 = f32[16,2,1,1,128]{3,4,1,0,2:T(8,128)} copy(f32[16,2,1,1,128]{4,0,3,2,1:T(8,128)S(1)} %bitcast.319) | data formatting | bytes 32768 | tf_op jit(solution)/shard_map/jit(_roll_static)/concatenate | solution.py:113
  151.6 10.6 %sqrt_bitcast_fusion = f32[16,2,128,128]{2,3,1,0:T(8,128)} fusion(f32[16,2,1,128,127]{3,4,1,0,2:T(8,128)} %bitcast.305, f32[16,2,1,128,1]{3,4,1,0,2:T(1,128)S(1)} %bitcast.316, f32[16,2,1,127,128]{3,4,1,0,2:T(8,128)} %get-tuple-element.22, f32[16,2,1,1,128]{3,4,1,0,2:T(8,128)} %copy.103, f32[16,2,1,128,1]{3,4,1,0,2:T(1,128)S(1)} %bitcast.315, ...), kind=kLoop, calls=%fused_computation.38 | loop fusion | flops 11010048 | bytes 23068800 | tf_op jit(solution)/shard_map/mul | solution.py:117
  162.2 4.3 %fusion.24 = bf16[1,16,2,2,128,128]{4,5,2,1,3,0:T(8,128)(2,1)S(1)} fusion(bf16[1,2,128,128]{3,2,1,0:T(8,128)(2,1)S(1)} %get-tuple-element.45, bf16[1,2,128,128]{3,2,1,0:T(8,128)(2,1)S(1)} %get-tuple-element.46, f32[16,2,2,128,128]{3,4,1,0,2:T(8,128)} %convolution_bitcast_fusion, f32[16,2,128,128]{2,3,1,0:T(8,128)} %sqrt_bitcast_fusion), kind=kOutput, calls=%fused_computation.54 | convolution fusion | flops 1078460416 | bytes 8519680 | tf_op jit(solution)/shard_map/npeuj,cvej->npcuv/dot_general | solution.py:48
  166.5 2.6 %copy.109 = bf16[1,16,2,2,128,128]{5,4,3,2,1,0:T(8,128)(2,1)} copy(bf16[1,16,2,2,128,128]{4,5,2,1,3,0:T(8,128)(2,1)S(1)} %fusion.24) | data formatting | bytes 4194304 | tf_op jit(solution)/shard_map/broadcast_in_dim | solution.py:175
  (30 shorter events, 0.4 us)
Async XLA Ops:
  0.0 2.6 %copy-start.5 = (f32[2,8192]{1,0:T(2,128)S(1)}, f32[2,8192]{1,0:T(2,128)}, u32[]{:S(2)}) copy-start(f32[2,8192]{1,0:T(2,128)} %param.7) | copy-start | bytes 196612
  4.2 10.8 %copy-start.6 = (s32[1,64]{1,0:T(1,128)S(1)}, s32[1,64]{1,0:T(1,128)}, u32[]{:S(2)}) copy-start(s32[1,64]{1,0:T(1,128)} %param.9) | copy-start | bytes 772
  8.2 22.5 %copy-start.4 = (bf16[2,128,1024]{2,1,0:T(8,128)(2,1)S(1)}, bf16[2,128,1024]{2,1,0:T(8,128)(2,1)}, u32[]{:S(2)}) copy-start(bf16[2,128,1024]{2,1,0:T(8,128)(2,1)} %param.8) | copy-start | bytes 1572868
  10.2 20.2 %all-to-all-start = ((bf16[8,2,16,1024]{3,2,1,0:T(8,128)(2,1)}), bf16[8,2,16,1024]{3,2,1,0:T(8,128)(2,1)S(1)}, u32[]{:S(2)}, u32[]{:S(2)}) async-start(bf16[8,2,16,1024]{3,2,1,0:T(8,128)(2,1)} %fusion.129), calls=%async_computation | async-start | bytes 1048576 | tf_op jit(solution)/shard_map/all_to_all | solution.py:129
  31.9 5.6 %copy-start.7 = (s32[1,64]{1,0:T(1,128)S(1)}, s32[1,64]{1,0:T(1,128)}, u32[]{:S(2)}) copy-start(s32[1,64]{1,0:T(1,128)} %param.10) | copy-start | bytes 772
  31.9 5.6 %copy-start.8 = (s32[1,64]{1,0:T(1,128)S(1)}, s32[1,64]{1,0:T(1,128)}, u32[]{:S(2)}) copy-start(s32[1,64]{1,0:T(1,128)} %param.11) | copy-start | bytes 772
  33.9 30.1 %all-to-all-start.1 = ((bf16[8,2,2,128,128]{4,1,3,2,0:T(2,128)(2,1)}), bf16[8,2,2,128,128]{4,1,3,2,0:T(2,128)(2,1)S(1)}, u32[]{:S(2)}, u32[]{:S(2)}) async-start(bf16[8,2,2,128,128]{4,1,3,2,0:T(2,128)(2,1)} %copy.82), calls=%async_computation.1 | async-start | bytes 2097152 | tf_op jit(solution)/shard_map/all_to_all | solution.py:159
  65.8 25.8 %collective-permute-start = (bf16[16,2,128,128]{2,3,1,0:T(8,128)(2,1)S(1)}, bf16[16,2,128,128]{2,3,1,0:T(8,128)(2,1)S(1)}, u32[]{:S(2)}, u32[]{:S(2)}) collective-permute-start(bf16[16,2,128,128]{2,3,1,0:T(8,128)(2,1)S(1)} %fusion.35), channel_id=1, source_target_pairs={{0,24},{8,0},{16,8},{24,16},{1,25},{9,1},{17,9},{25,17},{2,26},{10... | collective-permute-start | bytes 3145736 | tf_op jit(solution)/shard_map/ppermute | solution.py:17
  66.5 46.8 %collective-permute-start.1 = (bf16[16,2,128,128]{2,3,1,0:T(8,128)(2,1)S(1)}, bf16[16,2,128,128]{2,3,1,0:T(8,128)(2,1)S(1)}, u32[]{:S(2)}, u32[]{:S(2)}) collective-permute-start(bf16[16,2,128,128]{2,3,1,0:T(8,128)(2,1)S(1)} %fusion.35), channel_id=1, source_target_pairs={{0,16},{8,24},{16,0},{24,8},{1,17},{9,25},{17,1},{25,9},{2,18},{10... | collective-permute-start | bytes 3145736 | tf_op jit(solution)/shard_map/ppermute | solution.py:17
  123.6 1.4 copy-start.2
  123.6 4.7 %copy-start.1 = (f32[16,2,127,128]{2,3,1,0:T(8,128)}, f32[16,2,127,128]{2,3,1,0:T(8,128)S(1)}, u32[]{:S(2)}) copy-start(f32[16,2,127,128]{2,3,1,0:T(8,128)S(1)} %get-tuple-element.23) | copy-start | bytes 6242308
  124.3 4.0 %copy-start = (f32[16,2,1,128]{2,3,1,0:T(8,128)}, f32[16,2,1,128]{2,3,1,0:T(8,128)S(1)}, u32[]{:S(2)}) copy-start(f32[16,2,1,128]{2,3,1,0:T(8,128)S(1)} %get-tuple-element.26) | copy-start | bytes 49156
  147.6 4.0 %copy-start.3 = (f32[16,2,128,127]{2,3,1,0:T(8,128)S(1)}, f32[16,2,128,127]{2,3,1,0:T(8,128)}, u32[]{:S(2)}) copy-start(f32[16,2,128,127]{2,3,1,0:T(8,128)} %get-tuple-element.5) | copy-start | bytes 6242308
